TPU v7x, 32 devices: a whole 2x2x4 slice. The times are simulated.
32 devices in a mesh: line: 8 (over z, y), bus: 4 (over x, core).
Axes of the slice: x: 2, y: 2, z: 4, core: 2. Of those that a mesh axis runs over, the one named last changes fastest.
Arguments:
- clearness: float32 [192, 8192], P(None, ('line', 'bus')), may hold values from 0.05 to 0.8
- cos_zenith: float32 [192, 8192], P(None, ('line', 'bus')), may hold values from 0.05 to 1
- sun_azimuth: float32 [192, 8192], P(None, ('line', 'bus')), may hold values from -3.140625 to 3.140625
- dirint_cell: int32 [192, 8192], P(None, ('line', 'bus')), may hold values from 0 to 1259
- sky_bin: int32 [192, 8192], P(None, ('line', 'bus')), may hold values from 0 to 7
- dirint_coef: float32 [1260], replicated, may hold values from 0.5 to 1.5
- perez_coef: float32 [6, 8], replicated, may hold values from -0.3 to 0.6
- tilt_class: int32 [8192], P(('line', 'bus')), may hold values from 0 to 7
- azimuth_class: int32 [8192], P(('line', 'bus')), may hold values from 0 to 11
- tilt_table: float32 [8], replicated, may hold values from 0 to 1
- azimuth_table: float32 [12], replicated, may hold values from -3.140625 to 3.140625
- capacity: float32 [8192], P(('line', 'bus')), may hold values from 0.2 to 2
- site_bus: int32 [8192], P(('line', 'bus')), may hold values from 0 to 70143, as said below
- transfer_factors: bfloat16 [16000, 70144], P('line', 'bus'), may hold values from -0.0234375 to 0.0234375
Outputs:
- flows: float32 [16000, 192], P('line', 'bus')
Inputs may be any that keep to these rules, and one draw needn't show every extreme that they name: `site_bus`: bus b lies in group b // 2192. In every aligned block of 256 sites at most 16 sites connect to buses of one group, and one group receives exactly 16 sites from every block.
All inputs are finite; a program needn't handle non-finite values.
Results may differ from a plain program's by a relative error of at most 0.0034.
Values may be sent and summed in bfloat16 or wider, within the bound.
No kernel may reach another device: no remote copies, remote signals or barrier semaphores. Data moves between devices by JAX's collectives and lax.ppermute only.
A program may use at most 128 MiB of HBM per device.

v0:
```python
import math
import jax
import jax.numpy as jnp
from jax import lax
from jax.sharding import PartitionSpec as P

BUSES = 70144
TILTS = 8
AZIMS = 12
solar_constant = 1367.0
albedo = 0.2
cos_limit = 0.08716
row_width = 36


def pick_table(classes, table, count):
    picked = jnp.zeros(classes.shape, jnp.float32)
    for entry in range(count):
        picked = jnp.where(classes == entry, table[entry], picked)
    return picked


def dirint_lookup(cell, dirint_coef):
    row_count = dirint_coef.shape[0] // row_width
    table = dirint_coef.reshape(row_count, row_width)
    flat_cell = cell.reshape(-1)
    upper = flat_cell // row_width
    lower = flat_cell % row_width
    row_pick = (upper[:, None] == jnp.arange(row_count, dtype=jnp.int32)[None, :]).astype(
        jnp.float32
    )
    rows = jnp.dot(
        row_pick, table, precision=lax.Precision.HIGHEST, preferred_element_type=jnp.float32
    )
    column_hit = lower[:, None] == jnp.arange(row_width, dtype=jnp.int32)[None, :]
    picked = jnp.sum(jnp.where(column_hit, rows, 0.0), axis=1)
    return picked.reshape(cell.shape)


def site_power(
    clear,
    cosz,
    sun_az,
    cell,
    sky,
    tilt_angle,
    array_azimuth,
    site_capacity,
    dirint_coef,
    perez_coef,
):
    global_flat = clear * solar_constant * cosz
    zenith = jnp.arccos(cosz)
    airmass = 1.0 / (cosz + 0.50572 * (96.07995 - zenith * (180.0 / math.pi)) ** (-1.6364))
    clear_beam = (
        0.866 - 0.122 * airmass + 0.0121 * airmass**2 - 0.000653 * airmass**3 + 1.4e-05 * airmass**4
    )
    part_a = 0.512 - 1.56 * clear + 2.286 * clear**2 - 2.222 * clear**3
    part_b = 0.37 + 0.962 * clear
    part_c = -0.28 + 0.932 * clear - 2.048 * clear**2
    beam_index = jnp.maximum(clear_beam - (part_a + part_b * jnp.exp(part_c * airmass)), 0.0)
    direct_normal = solar_constant * beam_index * dirint_lookup(cell, dirint_coef)
    diffuse = jnp.maximum(global_flat - direct_normal * cosz, 0.1 * global_flat)
    brightness = diffuse * airmass / solar_constant
    factors = [jnp.zeros(cosz.shape, jnp.float32) for entry in range(6)]
    for bin_index in range(perez_coef.shape[1]):
        hit = sky == bin_index
        factors = [jnp.where(hit, perez_coef[row, bin_index], factors[row]) for row in range(6)]
    circumsolar = jnp.maximum(0.0, factors[0] + factors[1] * brightness + factors[2] * zenith)
    horizon_term = factors[3] + factors[4] * brightness + factors[5] * zenith
    cos_tilt = jnp.cos(tilt_angle)
    sin_tilt = jnp.sin(tilt_angle)
    cos_incidence = cosz * cos_tilt + jnp.sin(zenith) * sin_tilt * jnp.cos(sun_az - array_azimuth)
    facing = jnp.maximum(cos_incidence, 0.0)
    horizon_cos = jnp.maximum(cosz, cos_limit)
    sky_part = diffuse * (
        (1.0 - circumsolar) * (1.0 + cos_tilt) * 0.5
        + circumsolar * facing / horizon_cos
        + horizon_term * sin_tilt
    )
    plane = direct_normal * facing + sky_part + albedo * global_flat * (1.0 - cos_tilt) * 0.5
    return (site_capacity * plane / 1000.0).astype(jnp.bfloat16)


def per_device(
    clearness,
    cos_zenith,
    sun_azimuth,
    dirint_cell,
    sky_bin,
    dirint_coef,
    perez_coef,
    tilt_class,
    azimuth_class,
    tilt_table,
    azimuth_table,
    capacity,
    site_bus,
    transfer_factors,
):
    line_count = lax.axis_size("line")
    bus_count = lax.axis_size("bus")
    owners = line_count * bus_count
    n_hours, n_sites = clearness.shape
    group_buses = BUSES // owners
    slots_each = max(2, 2 * n_sites // owners)
    tilt_angle = pick_table(tilt_class, tilt_table, TILTS)
    array_azimuth = pick_table(azimuth_class, azimuth_table, AZIMS)
    power = site_power(
        clearness,
        cos_zenith,
        sun_azimuth,
        dirint_cell,
        sky_bin,
        tilt_angle,
        array_azimuth,
        capacity,
        dirint_coef,
        perez_coef,
    )
    group_index = site_bus // group_buses
    target = group_index % line_count * bus_count + group_index // line_count
    local_bus = site_bus % group_buses
    one_hot = (target[:, None] == jnp.arange(owners, dtype=jnp.int32)[None, :]).astype(jnp.int32)
    position = jnp.sum(one_hot * (jnp.cumsum(one_hot, axis=0) - 1), axis=1)
    slot_index = target * slots_each + position
    outgoing = jnp.zeros((n_hours, owners * slots_each), jnp.bfloat16).at[:, slot_index].set(power)
    labels = jnp.zeros((1, owners * slots_each), jnp.int32).at[0, slot_index].set(local_bus)
    arrived, bus_tags = (
        lax.all_to_all(outgoing, ("line", "bus"), split_axis=1, concat_axis=1, tiled=True),
        lax.all_to_all(labels, ("line", "bus"), split_axis=1, concat_axis=1, tiled=True),
    )
    bus_tags = bus_tags.reshape(owners * slots_each)
    member = (bus_tags[:, None] == jnp.arange(group_buses, dtype=jnp.int32)[None, :]).astype(
        jnp.bfloat16
    )
    injection = jnp.einsum("hr,rb->bh", arrived, member, preferred_element_type=jnp.float32).astype(
        jnp.bfloat16
    )
    partial_flows = jnp.dot(
        transfer_factors,
        lax.all_gather(injection, "line", axis=0, tiled=True),
        preferred_element_type=jnp.float32,
    )
    return lax.psum_scatter(partial_flows, "bus", scatter_dimension=1, tiled=True)


def solution(mesh):
    in_specs = (
        P(None, ("line", "bus")),
        P(None, ("line", "bus")),
        P(None, ("line", "bus")),
        P(None, ("line", "bus")),
        P(None, ("line", "bus")),
        P(),
        P(),
        P(("line", "bus")),
        P(("line", "bus")),
        P(),
        P(),
        P(("line", "bus")),
        P(("line", "bus")),
        P("line", "bus"),
    )
    out_specs = P("line", "bus")
    return jax.shard_map(
        per_device, mesh=mesh, in_specs=in_specs, out_specs=out_specs, check_vma=False
    )
```

profile of v0, /device:TPU:0, one launch (start us, length us, event | category | flops | bytes accessed | tf_op | source)
XLA Modules:
  0.0 296.3 jit_solution(16229938110226175644)
XLA Ops:
  6.5 0.0 copy-start.2
  6.6 0.8 and_select_fusion
  7.3 0.6 reduce-window.6
  7.9 0.2 slice_reduce_fusion
  8.2 0.1 fusion.27
  8.3 1.4 scatter_custom_fusion
  9.7 0.7 all_to_all.14
  10.4 7.3 %all-to-all-start = ((s32[1,32,16]{2,0,1:T(1,128)}), s32[1,32,16]{2,0,1:T(1,128)S(1)}, u32[]{:S(2)}, u32[]{:S(2)}) async-start(s32[1,32,16]{2,0,1:T(1,128)} %bitcast.2), calls=%async_computation | async-start | bytes 32768 | tf_op jit(solution)/shard_map/all_to_all | solution.py:131
  17.7 1.7 fusion.36
  19.4 2.1 fusion.34
  21.5 2.1 fusion.35
  23.6 1.0 sign_compare_fusion
  24.6 1.0 remainder_bitcast_fusion
  25.6 1.6 fusion.38
  27.2 5.7 %fusion.33 = (f32[256]{0:T(256)S(1)}, f32[256]{0:T(256)S(1)}) fusion(f32[]{:T(128)} %bitcast.10, s32[256]{0:T(256)} %param.21, f32[]{:T(128)} %bitcast.9, f32[]{:T(128)} %bitcast.8, f32[]{:T(128)} %bitcast.7, f32[]{:T(128)} %bitcast.6, f32[]{:T(128)} %bitcast.5, f32[]{:T(128)} %bitcast.4, f32[]{:T(128)} %bitcast.3), kind=kLoop, calls=%fused_computation.89 | loop fusion | flops 4096 | bytes 3104 | tf_op jit(solution)/shard_map/sin | solution.py:72
  33.0 1.8 fusion.37
  34.8 0.8 reshape.70
  35.7 0.1 copy.28
  35.8 0.1 copy.29
  35.9 0.1 add_select_fusion.1
  36.0 5.6 %fusion.5 = f32[49152]{0:T(1024)S(1)} fusion(f32[35,36]{1,0:T(8,128)S(1)} %reshape.70, s32[49152]{0:T(1024)S(1)} %get-tuple-element.8, s32[49152]{0:T(1024)S(1)} %get-tuple-element.7), kind=kOutput, calls=%fused_computation.12 | convolution fusion | flops 750157824 | bytes 594864 | tf_op jit(solution)/shard_map/dot_general | solution.py:32
  41.6 0.1 reshape.71
  41.7 0.0 copy-done.4
  41.7 7.5 %broadcast_add_fusion = (f32[256]{0:T(256)S(1)}, f32[256]{0:T(256)S(1)}, f32[256]{0:T(256)S(1)}) fusion(f32[256]{0:T(256)S(1)} %cos.6, f32[]{:T(128)} %bitcast.22, s32[256]{0:T(256)S(1)} %copy-done.4, f32[]{:T(128)} %bitcast.21, f32[]{:T(128)} %bitcast.20, f32[]{:T(128)} %bitcast.19, f32[]{:T(128)} %bitcast.18, f32[]{:T(128)} %bitcast.17, f32[]{:T(128)} %bitcast.16, ...), kind=kLoop, calls=%fused_computation.88 | loop fusion | flops 6912 | bytes 5168 | tf_op jit(solution)/shard_map/add | solution.py:77
  49.2 0.0 copy-done.5
  49.2 0.0 copy-done.1
  49.2 0.0 copy-done.3
  49.2 0.0 copy-done
  49.3 0.0 copy-done.2
  49.3 32.6 %fusion.25 = bf16[256,192]{0,1:T(8,128)(2,1)S(1)} fusion(f32[256]{0:T(256)S(1)} %get-tuple-element.62, f32[]{:T(128)} %bitcast.70, f32[]{:T(128)} %bitcast.69, f32[]{:T(128)} %bitcast.68, f32[]{:T(128)} %bitcast.67, f32[]{:T(128)} %bitcast.66, f32[]{:T(128)} %bitcast.65, f32[]{:T(128)} %bitcast.64, f32[]{:T(128)} %bitcast.63, f32[]{:T(128)} %bitcast.62, ...), kind=kLoop, calls=%fused_computation.45 | loop fusion | flops 6733824 | bytes 1087680 | tf_op jit(solution)/shard_map/convert_element_type | solution.py:82
  81.8 0.1 copy.25
  81.9 2.1 scatter_custom_fusion.1
  84.1 0.0 all-to-all-done
  84.1 5.8 %all-to-all-start.1 = ((bf16[192,32,16]{0,2,1:T(8,128)(2,1)}), bf16[192,32,16]{0,2,1:T(8,128)(2,1)S(1)}, u32[]{:S(2)}, u32[]{:S(2)}) async-start(bf16[192,32,16]{0,2,1:T(8,128)(2,1)} %bitcast.72), calls=%async_computation.1 | async-start | bytes 524288 | tf_op jit(solution)/shard_map/all_to_all | solution.py:130
  89.9 0.0 all-gather.3.cloned.1.call-start
  90.0 0.5 broadcast.198
  90.5 0.7 reduce.5
  91.2 0.1 eq.192
  91.3 9.2 %all-to-all-done.1 = bf16[192,32,16]{0,2,1:T(8,128)(2,1)S(1)} async-done(((bf16[192,32,16]{0,2,1:T(8,128)(2,1)}), bf16[192,32,16]{0,2,1:T(8,128)(2,1)S(1)}, u32[]{:S(2)}, u32[]{:S(2)}) %all-to-all-start.1) | async-done | bytes 196640 | tf_op jit(solution)/shard_map/all_to_all | solution.py:130
  100.5 2.1 fusion.3
  102.6 0.0 all-gather.3.cloned.1.call-update
  102.7 0.2 reduce-scatter.2.cloned.1.call-start
  102.9 106.5 %all-gather.3.cloned.1.call-done = bf16[8,2192,192]{1,2,0:T(8,128)(2,1)} async-done(((bf16[1,2192,192]{1,2,0:T(8,128)(2,1)}), bf16[8,2192,192]{1,2,0:T(8,128)(2,1)}) %all-gather.3.cloned.1.call-update) | async-done | bytes 6733840 | tf_op jit(solution)/shard_map/all_gather | solution.py:142
  209.4 9.8 %copy.26 = bf16[8,2192,192]{1,0,2:T(8,128)(2,1)} copy(bf16[8,2192,192]{1,2,0:T(8,128)(2,1)} %all-gather.3.cloned.1.call-done) | data formatting | bytes 13467648 | tf_op jit(solution)/shard_map/all_gather | solution.py:142
  219.3 12.5 %reshape.97 = bf16[17536,192]{0,1:T(8,128)(2,1)} reshape(bf16[8,2192,192]{1,0,2:T(8,128)(2,1)} %copy.26) | data formatting | bytes 13467648
  231.8 31.1 %convolution_bitcast_fusion = f32[2000,192]{0,1:T(8,128)} fusion(bf16[17536,192]{0,1:T(8,128)(2,1)} %reshape.97, bf16[2000,17536]{1,0:T(8,128)(2,1)} %param.27), kind=kOutput, calls=%fused_computation.10 | convolution fusion | flops 13467648000 | bytes 78413824 | tf_op jit(solution)/shard_map/dot_general | solution.py:140
  262.9 0.0 reduce-scatter.2.cloned.1.call-update
  262.9 26.5 %reduce-scatter.2.cloned.1.call-done = f32[2000,48]{0,1:T(8,128)} async-done(((f32[2000,192]{0,1:T(8,128)}), f32[2000,48]{0,1:T(8,128)}) %reduce-scatter.2.cloned.1.call-update) | async-done | bytes 384016 | tf_op jit(solution)/shard_map/reduce_scatter | solution.py:145
  (11 shorter events, 0.1 us)
Async XLA Ops:
  6.5 35.2 %copy-start.4 = (s32[256]{0:T(256)S(1)}, s32[256]{0:T(256)}, u32[]{:S(2)}) copy-start(s32[256]{0:T(256)} %param.22) | copy-start | bytes 3076
  6.5 42.7 %copy-start.5 = (f32[256]{0:T(256)S(1)}, f32[256]{0:T(256)}, u32[]{:S(2)}) copy-start(f32[256]{0:T(256)} %param.25) | copy-start | bytes 3076
  6.5 42.7 %copy-start.1 = (s32[192,256]{1,0:T(8,128)S(1)}, s32[192,256]{1,0:T(8,128)}, u32[]{:S(2)}) copy-start(s32[192,256]{1,0:T(8,128)} %param.18) | copy-start | bytes 589828
  6.5 42.7 %copy-start.3 = (f32[192,256]{1,0:T(8,128)S(1)}, f32[192,256]{1,0:T(8,128)}, u32[]{:S(2)}) copy-start(f32[192,256]{1,0:T(8,128)} %param.16) | copy-start | bytes 589828
  6.5 42.7 %copy-start = (f32[192,256]{1,0:T(8,128)S(1)}, f32[192,256]{1,0:T(8,128)}, u32[]{:S(2)}) copy-start(f32[192,256]{1,0:T(8,128)} %param.15) | copy-start | bytes 589828
  6.5 42.7 %copy-start.2 = (f32[192,256]{1,0:T(8,128)S(1)}, f32[192,256]{1,0:T(8,128)}, u32[]{:S(2)}) copy-start(f32[192,256]{1,0:T(8,128)} %param.14) | copy-start | bytes 589828
  10.4 73.7 %all-to-all-start = ((s32[1,32,16]{2,0,1:T(1,128)}), s32[1,32,16]{2,0,1:T(1,128)S(1)}, u32[]{:S(2)}, u32[]{:S(2)}) async-start(s32[1,32,16]{2,0,1:T(1,128)} %bitcast.2), calls=%async_computation | async-start | bytes 32768 | tf_op jit(solution)/shard_map/all_to_all | solution.py:131
  84.1 16.4 %all-to-all-start.1 = ((bf16[192,32,16]{0,2,1:T(8,128)(2,1)}), bf16[192,32,16]{0,2,1:T(8,128)(2,1)S(1)}, u32[]{:S(2)}, u32[]{:S(2)}) async-start(bf16[192,32,16]{0,2,1:T(8,128)(2,1)} %bitcast.72), calls=%async_computation.1 | async-start | bytes 524288 | tf_op jit(solution)/shard_map/all_to_all | solution.py:130
  89.9 119.5 %all-gather.3.cloned.1.call-start = ((), (), s32[]{:S(2)}) async-start(), calls=%async_computation.4 | async-start | bytes 7962624 | tf_op jit(solution)/shard_map/all_gather | solution.py:142
  102.7 186.8 %reduce-scatter.2.cloned.1.call-start = ((), (), s32[]{:S(2)}) async-start(), calls=%async_computation.3 | async-start | bytes 1966080 | tf_op jit(solution)/shard_map/reduce_scatter | solution.py:145
Sparse Core Ops, SparseCore 0:
  102.8 106.5 all-gather.2
  263.0 26.3 reduce-scatter.1
where the time goes:
time: 298 us; the launch traced here: 296 us
  waiting for transfers between devices  142 us (48%)
  other arithmetic  50.1 us (17%)
  matrix products  38.8 us (13%)
  local copies, waits for them, and re-layouts  38 us (13%)
  between operations  13.6 us (5%)
  starting transfers between devices  13.4 us (4%)
    all_gather x1, waiting for transfers between devices, per_device(): lax.all_gather(injection, 'line', axis=0, tiled=True)  107 us
    convert_element_type x1, other arithmetic, site_power(): return (site_capacity * plane / 1000.0).astype(jnp.bfloat16)  32.6 us
    dot_general x1, matrix products, per_device(): jnp.dot(transfer_factors, lax.all_gather(injection, 'line', axis=0, tiled...  31.1 us
    reduce_scatter x1, waiting for transfers between devices, per_device(): lax.psum_scatter(partial_flows, 'bus', scatter_dimension=1, tiled=True)  26.5 us
    unnamed x15, local copies, waits for them, and re-layouts  12.8 us
    all_gather x1, local copies, waits for them, and re-layouts, per_device(): lax.all_gather(injection, 'line', axis=0, tiled=True)  9.83 us
    all_to_all x1, waiting for transfers between devices, per_device(): lax.all_to_all(outgoing, ('line', 'bus'), split_axis=1, concat_axis=1, ti...  9.25 us
    add x1, other arithmetic, site_power(): 1.0 + cos_tilt  7.51 us
  transfers between devices with their start and end apart: 4, of which 3 were waited for; matrix products, arithmetic and copies ran while one was open for 23% of the time, Pallas kernels for 0%

commit v1 on v0

--- a/solution.py
+++ b/solution.py
@@ -11,6 +11,35 @@
 albedo = 0.2
 cos_limit = 0.08716
 row_width = 36
+
+
+def follow_groups(own_rows):
+    outcome_arr, back, piece_next = (
+        jax.lax.axis_size("line"),
+        jax.lax.axis_index("line"),
+        own_rows.shape[0],
+    )
+    pile = [(rr, (rr + 1) % outcome_arr) for rr in range(outcome_arr)]
+    stack_in = [(rr, (rr - 1) % outcome_arr) for rr in range(outcome_arr)]
+    value_now = jnp.zeros(
+        (*own_rows.shape[:0], outcome_arr * piece_next, *own_rows.shape[1:]), own_rows.dtype
+    )
+    value_now = lax.dynamic_update_slice_in_dim(value_now, own_rows, back * piece_next, axis=0)
+    current_arr = built = own_rows
+    finding = outcome_arr // 2
+    c = 1
+    while c < finding + 1:
+        current_arr = jax.lax.ppermute(current_arr, "line", pile)
+        value_now = lax.dynamic_update_slice_in_dim(
+            value_now, current_arr, (back - c) % outcome_arr * piece_next, axis=0
+        )
+        if c < outcome_arr - finding:
+            built = jax.lax.ppermute(built, "line", stack_in)
+            value_now = lax.dynamic_update_slice_in_dim(
+                value_now, built, (back + c) % outcome_arr * piece_next, axis=0
+            )
+        c += 1
+    return value_now
 
 
 def pick_table(classes, table, count):
@@ -138,9 +167,7 @@
         jnp.bfloat16
     )
     partial_flows = jnp.dot(
-        transfer_factors,
-        lax.all_gather(injection, "line", axis=0, tiled=True),
-        preferred_element_type=jnp.float32,
+        transfer_factors, follow_groups(injection), preferred_element_type=jnp.float32
     )
     return lax.psum_scatter(partial_flows, "bus", scatter_dimension=1, tiled=True)
 

time: 298 us -> 362 us (1.21)
  local copies, waits for them, and re-layouts: 38 us -> 88.5 us
  starting transfers between devices: 13.4 us -> 29.9 us
    all_gather x1 -> x0, waiting for transfers between devices: 107 us -> none  [per_device(): lax.all_gather(injection, 'line', axis=0, tiled=True)]
    ppermute x0 -> x7, waiting for transfers between devices: none -> 102 us  [the longest x4 102 us: follow_groups(): current_arr = jax.lax.ppermute(current_arr, 'line', pile)]
    dynamic_update_slice x0 -> x8, local copies, waits for them, and re-layouts: none -> 69.6 us  [the longest x4 34.8 us: follow_groups(): lax.dynamic_update_slice_in_dim(value_now, current_arr, (back - c) % outc...]
    ppermute x0 -> x7, starting transfers between devices: none -> 16.7 us  [the longest x4 8.38 us: follow_groups(): current_arr = jax.lax.ppermute(current_arr, 'line', pile)]
    unnamed x15 -> x16, local copies, waits for them, and re-layouts: 12.8 us -> 0.23 us
    all_gather x1 -> x0, local copies, waits for them, and re-layouts: 9.83 us -> none  [per_device(): lax.all_gather(injection, 'line', axis=0, tiled=True)]
  transfers between devices with their start and end apart: 4 -> 10, of which waited for: 3 -> 5; matrix products, arithmetic and copies ran while one was open for 23% -> 37% of each run, Pallas kernels for 0% -> 0%
where the time goes in v1:
time: 362 us; the launch traced here: 359 us
  waiting for transfers between devices  139 us (38%)
  local copies, waits for them, and re-layouts  88.5 us (24%)
  other arithmetic  50.1 us (14%)
  matrix products  37.8 us (10%)
  starting transfers between devices  29.9 us (8%)
  between operations  13.6 us (4%)
    ppermute x4, waiting for transfers between devices, follow_groups(): current_arr = jax.lax.ppermute(current_arr, 'line', pile)  102 us
    dynamic_update_slice x4, local copies, waits for them, and re-layouts, follow_groups(): lax.dynamic_update_slice_in_dim(value_now, current_arr, (back - c) % outc...  34.8 us
    convert_element_type x1, other arithmetic, site_power(): return (site_capacity * plane / 1000.0).astype(jnp.bfloat16)  32.6 us
    dot_general x1, matrix products, per_device(): jnp.dot(transfer_factors, follow_groups(injection), preferred_element_typ...  31.1 us
    reduce_scatter x1, waiting for transfers between devices, per_device(): lax.psum_scatter(partial_flows, 'bus', scatter_dimension=1, tiled=True)  28.3 us
    dynamic_update_slice x3, local copies, waits for them, and re-layouts, follow_groups(): lax.dynamic_update_slice_in_dim(value_now, built, (back + c) % outcome_ar...  26.9 us
    all_to_all x1, waiting for transfers between devices, per_device(): lax.all_to_all(outgoing, ('line', 'bus'), split_axis=1, concat_axis=1, ti...  9.14 us
    ppermute x4, starting transfers between devices, follow_groups(): current_arr = jax.lax.ppermute(current_arr, 'line', pile)  8.38 us
  transfers between devices with their start and end apart: 10, of which 5 were waited for; matrix products, arithmetic and copies ran while one was open for 37% of the time, Pallas kernels for 0%

profile of v1, /device:TPU:0, one launch (start us, length us, event | category | flops | bytes accessed | tf_op | source)
XLA Modules:
  0.0 359.1 jit_solution(1913740389737753624)
XLA Ops:
  6.6 0.8 and_select_fusion
  7.3 0.6 reduce-window.6
  7.9 0.2 slice_reduce_fusion
  8.2 0.1 fusion.26
  8.3 1.4 scatter_custom_fusion
  9.7 0.7 all_to_all.14
  10.4 7.3 %all-to-all-start = ((s32[1,32,16]{2,0,1:T(1,128)}), s32[1,32,16]{2,0,1:T(1,128)S(1)}, u32[]{:S(2)}, u32[]{:S(2)}) async-start(s32[1,32,16]{2,0,1:T(1,128)} %bitcast.2), calls=%async_computation | async-start | bytes 32768 | tf_op jit(solution)/shard_map/all_to_all | solution.py:160
  17.7 2.1 fusion.33
  19.8 2.1 fusion.34
  21.9 1.7 fusion.35
  23.6 1.0 remainder_bitcast_fusion
  24.6 1.0 sign_compare_fusion
  25.6 1.6 fusion.37
  27.2 5.7 %fusion.32 = (f32[256]{0:T(256)S(1)}, f32[256]{0:T(256)S(1)}) fusion(f32[]{:T(128)} %bitcast.10, s32[256]{0:T(256)} %param.21, f32[]{:T(128)} %bitcast.9, f32[]{:T(128)} %bitcast.8, f32[]{:T(128)} %bitcast.7, f32[]{:T(128)} %bitcast.6, f32[]{:T(128)} %bitcast.5, f32[]{:T(128)} %bitcast.4, f32[]{:T(128)} %bitcast.3), kind=kLoop, calls=%fused_computation.88 | loop fusion | flops 4096 | bytes 3104 | tf_op jit(solution)/shard_map/sin | solution.py:101
  33.0 1.8 fusion.36
  34.8 0.1 copy.25
  34.9 0.1 copy.26
  35.0 0.8 reshape.70
  35.9 5.6 %fusion.4 = f32[49152]{0:T(1024)S(1)} fusion(f32[35,36]{1,0:T(8,128)S(1)} %reshape.70, s32[49152]{0:T(1024)S(1)} %get-tuple-element.8, s32[49152]{0:T(1024)S(1)} %get-tuple-element.7), kind=kOutput, calls=%fused_computation.11 | convolution fusion | flops 750157824 | bytes 594864 | tf_op jit(solution)/shard_map/dot_general | solution.py:61
  41.6 7.5 %broadcast_add_fusion = (f32[256]{0:T(256)S(1)}, f32[256]{0:T(256)S(1)}, f32[256]{0:T(256)S(1)}) fusion(f32[256]{0:T(256)S(1)} %cos.6, f32[]{:T(128)} %bitcast.22, s32[256]{0:T(256)S(1)} %copy-done.5, f32[]{:T(128)} %bitcast.21, f32[]{:T(128)} %bitcast.20, f32[]{:T(128)} %bitcast.19, f32[]{:T(128)} %bitcast.18, f32[]{:T(128)} %bitcast.17, f32[]{:T(128)} %bitcast.16, ...), kind=kLoop, calls=%fused_computation.87 | loop fusion | flops 6912 | bytes 5168 | tf_op jit(solution)/shard_map/add | solution.py:106
  49.2 32.6 %fusion.24 = bf16[256,192]{0,1:T(8,128)(2,1)S(1)} fusion(f32[256]{0:T(256)S(1)} %get-tuple-element.62, f32[]{:T(128)} %bitcast.70, f32[]{:T(128)} %bitcast.69, f32[]{:T(128)} %bitcast.68, f32[]{:T(128)} %bitcast.67, f32[]{:T(128)} %bitcast.66, f32[]{:T(128)} %bitcast.65, f32[]{:T(128)} %bitcast.64, f32[]{:T(128)} %bitcast.63, f32[]{:T(128)} %bitcast.62, ...), kind=kLoop, calls=%fused_computation.44 | loop fusion | flops 6733824 | bytes 1087680 | tf_op jit(solution)/shard_map/convert_element_type | solution.py:111
  81.8 2.1 scatter_custom_fusion.1
  84.0 5.8 %all-to-all-start.1 = ((bf16[192,32,16]{0,2,1:T(8,128)(2,1)}), bf16[192,32,16]{0,2,1:T(8,128)(2,1)S(1)}, u32[]{:S(2)}, u32[]{:S(2)}) async-start(bf16[192,32,16]{0,2,1:T(8,128)(2,1)} %bitcast.72), calls=%async_computation.1 | async-start | bytes 524288 | tf_op jit(solution)/shard_map/all_to_all | solution.py:159
  89.9 0.6 broadcast.205
  90.5 0.7 reduce.5
  91.3 9.1 %all-to-all-done.1 = bf16[192,32,16]{0,2,1:T(8,128)(2,1)S(1)} async-done(((bf16[192,32,16]{0,2,1:T(8,128)(2,1)}), bf16[192,32,16]{0,2,1:T(8,128)(2,1)S(1)}, u32[]{:S(2)}, u32[]{:S(2)}) %all-to-all-start.1) | async-done | bytes 196640 | tf_op jit(solution)/shard_map/all_to_all | solution.py:159
  100.4 1.2 fusion.2
  101.6 0.9 collective-permute-start
  102.6 3.8 %collective-permute-start.1 = (bf16[2192,192]{0,1:T(8,128)(2,1)S(1)}, bf16[2192,192]{0,1:T(8,128)(2,1)S(1)}, u32[]{:S(2)}, u32[]{:S(2)}) collective-permute-start(bf16[2192,192]{0,1:T(8,128)(2,1)S(1)} %fusion.2), channel_id=1, source_target_pairs={{0,28},{4,0},{8,4},{12,8},{16,12},{20,16},{24,20},{28,24},{1,29},{... | collective-permute-start | bytes 2525192 | tf_op jit(solution)/shard_map/ppermute | solution.py:37
  106.4 33.5 %collective-permute-done = bf16[2192,192]{0,1:T(8,128)(2,1)S(1)} collective-permute-done((bf16[2192,192]{0,1:T(8,128)(2,1)S(1)}, bf16[2192,192]{0,1:T(8,128)(2,1)S(1)}, u32[]{:S(2)}, u32[]{:S(2)}) %collective-permute-start) | collective-permute-done | bytes 841760 | tf_op jit(solution)/shard_map/ppermute | solution.py:32
  139.9 2.5 collective-permute-start.2
  142.4 2.2 collective-permute-start.3
  144.7 34.2 %collective-permute-done.2 = bf16[2192,192]{0,1:T(8,128)(2,1)S(1)} collective-permute-done((bf16[2192,192]{0,1:T(8,128)(2,1)S(1)}, bf16[2192,192]{0,1:T(8,128)(2,1)S(1)}, u32[]{:S(2)}, u32[]{:S(2)}) %collective-permute-start.2) | collective-permute-done | bytes 841760 | tf_op jit(solution)/shard_map/ppermute | solution.py:32
  178.8 2.5 collective-permute-start.4
  181.3 2.2 collective-permute-start.5
  183.6 34.0 %collective-permute-done.4 = bf16[2192,192]{0,1:T(8,128)(2,1)S(1)} collective-permute-done((bf16[2192,192]{0,1:T(8,128)(2,1)S(1)}, bf16[2192,192]{0,1:T(8,128)(2,1)S(1)}, u32[]{:S(2)}, u32[]{:S(2)}) %collective-permute-start.4) | collective-permute-done | bytes 841760 | tf_op jit(solution)/shard_map/ppermute | solution.py:32
  217.6 2.5 collective-permute-start.6
  220.1 3.2 broadcast_in_dim.238
  223.3 7.9 %dynamic_update_slice.24 = bf16[17536,192]{0,1:T(8,128)(2,1)} dynamic-update-slice(bf16[17536,192]{0,1:T(8,128)(2,1)} %broadcast_in_dim.238, bf16[2192,192]{0,1:T(8,128)(2,1)S(1)} %fusion.2, s32[]{:T(128)S(6)} %select_n.382, s32[]{:T(128)} %constant.87.clone.1) | dynamic-update-slice | bytes 1683460 | tf_op jit(solution)/shard_map/dynamic_update_slice | solution.py:27
  231.2 8.0 %dynamic_update_slice.25 = bf16[17536,192]{0,1:T(8,128)(2,1)} dynamic-update-slice(bf16[17536,192]{0,1:T(8,128)(2,1)} %dynamic_update_slice.24, bf16[2192,192]{0,1:T(8,128)(2,1)S(1)} %collective-permute-done, s32[]{:T(128)S(6)} %select_n.384, s32[]{:T(128)} %constant.87.clone.1) | dynamic-update-slice | bytes 1683460 | tf_op jit(solution)/shard_map/dynamic_update_slice | solution.py:33
  239.2 8.7 %dynamic_update_slice.26 = bf16[17536,192]{0,1:T(8,128)(2,1)} dynamic-update-slice(bf16[17536,192]{0,1:T(8,128)(2,1)} %dynamic_update_slice.25, bf16[2192,192]{0,1:T(8,128)(2,1)S(1)} %collective-permute-done.1, s32[]{:T(128)S(6)} %select_n.386, s32[]{:T(128)} %constant.87.clone.1) | dynamic-update-slice | bytes 1683460 | tf_op jit(solution)/shard_map/dynamic_update_slice | solution.py:38
  247.9 9.0 %dynamic_update_slice.27 = bf16[17536,192]{0,1:T(8,128)(2,1)} dynamic-update-slice(bf16[17536,192]{0,1:T(8,128)(2,1)} %dynamic_update_slice.26, bf16[2192,192]{0,1:T(8,128)(2,1)} %copy-done, s32[]{:T(128)S(6)} %select_n.388, s32[]{:T(128)} %constant.87.clone.1) | dynamic-update-slice | bytes 1683460 | tf_op jit(solution)/shard_map/dynamic_update_slice | solution.py:33
  256.9 9.1 %dynamic_update_slice.28 = bf16[17536,192]{0,1:T(8,128)(2,1)} dynamic-update-slice(bf16[17536,192]{0,1:T(8,128)(2,1)} %dynamic_update_slice.27, bf16[2192,192]{0,1:T(8,128)(2,1)} %collective-permute-done.3, s32[]{:T(128)S(6)} %select_n.390, s32[]{:T(128)} %constant.87.clone.1) | dynamic-update-slice | bytes 1683460 | tf_op jit(solution)/shard_map/dynamic_update_slice | solution.py:38
  266.0 8.7 %dynamic_update_slice.29 = bf16[17536,192]{0,1:T(8,128)(2,1)} dynamic-update-slice(bf16[17536,192]{0,1:T(8,128)(2,1)} %dynamic_update_slice.28, bf16[2192,192]{0,1:T(8,128)(2,1)S(1)} %collective-permute-done.4, s32[]{:T(128)S(6)} %select_n.392, s32[]{:T(128)} %constant.87.clone.1) | dynamic-update-slice | bytes 1683460 | tf_op jit(solution)/shard_map/dynamic_update_slice | solution.py:33
  274.7 9.1 %dynamic_update_slice.30 = bf16[17536,192]{0,1:T(8,128)(2,1)} dynamic-update-slice(bf16[17536,192]{0,1:T(8,128)(2,1)} %dynamic_update_slice.29, bf16[2192,192]{0,1:T(8,128)(2,1)} %collective-permute-done.5, s32[]{:T(128)S(6)} %select_n.394, s32[]{:T(128)} %constant.87.clone.1) | dynamic-update-slice | bytes 1683460 | tf_op jit(solution)/shard_map/dynamic_update_slice | solution.py:38
  283.8 9.1 %dynamic_update_slice.31 = bf16[17536,192]{0,1:T(8,128)(2,1)} dynamic-update-slice(bf16[17536,192]{0,1:T(8,128)(2,1)} %dynamic_update_slice.30, bf16[2192,192]{0,1:T(8,128)(2,1)} %collective-permute-done.6, s32[]{:T(128)S(6)} %select_n.396, s32[]{:T(128)} %constant.87.clone.1) | dynamic-update-slice | bytes 1683460 | tf_op jit(solution)/shard_map/dynamic_update_slice | solution.py:33
  292.9 31.1 %convolution_bitcast_fusion = f32[2000,192]{0,1:T(8,128)} fusion(bf16[17536,192]{0,1:T(8,128)(2,1)} %dynamic_update_slice.31, bf16[2000,17536]{1,0:T(8,128)(2,1)} %param.27), kind=kOutput, calls=%fused_computation.9 | convolution fusion | flops 13467648000 | bytes 78413824 | tf_op jit(solution)/shard_map/dot_general | solution.py:169
  324.0 28.3 %reduce-scatter.2.cloned.1.call-done = f32[2000,48]{0,1:T(8,128)} async-done(((f32[2000,192]{0,1:T(8,128)}), f32[2000,48]{0,1:T(8,128)}) %reduce-scatter.2.cloned.1.call-update) | async-done | bytes 384016 | tf_op jit(solution)/shard_map/reduce_scatter | solution.py:172
  (31 shorter events, 0.6 us)
Async XLA Ops:
  6.5 35.0 %copy-start.5 = (s32[256]{0:T(256)S(1)}, s32[256]{0:T(256)}, u32[]{:S(2)}) copy-start(s32[256]{0:T(256)} %param.22) | copy-start | bytes 3076
  6.5 42.6 %copy-start.3 = (f32[192,256]{1,0:T(8,128)S(1)}, f32[192,256]{1,0:T(8,128)}, u32[]{:S(2)}) copy-start(f32[192,256]{1,0:T(8,128)} %param.14) | copy-start | bytes 589828
  6.5 42.6 %copy-start.1 = (f32[192,256]{1,0:T(8,128)S(1)}, f32[192,256]{1,0:T(8,128)}, u32[]{:S(2)}) copy-start(f32[192,256]{1,0:T(8,128)} %param.15) | copy-start | bytes 589828
  6.5 42.6 %copy-start.4 = (f32[192,256]{1,0:T(8,128)S(1)}, f32[192,256]{1,0:T(8,128)}, u32[]{:S(2)}) copy-start(f32[192,256]{1,0:T(8,128)} %param.16) | copy-start | bytes 589828
  6.5 42.6 %copy-start.2 = (s32[192,256]{1,0:T(8,128)S(1)}, s32[192,256]{1,0:T(8,128)}, u32[]{:S(2)}) copy-start(s32[192,256]{1,0:T(8,128)} %param.18) | copy-start | bytes 589828
  6.5 42.6 %copy-start.6 = (f32[256]{0:T(256)S(1)}, f32[256]{0:T(256)}, u32[]{:S(2)}) copy-start(f32[256]{0:T(256)} %param.25) | copy-start | bytes 3076
  10.4 73.6 %all-to-all-start = ((s32[1,32,16]{2,0,1:T(1,128)}), s32[1,32,16]{2,0,1:T(1,128)S(1)}, u32[]{:S(2)}, u32[]{:S(2)}) async-start(s32[1,32,16]{2,0,1:T(1,128)} %bitcast.2), calls=%async_computation | async-start | bytes 32768 | tf_op jit(solution)/shard_map/all_to_all | solution.py:160
  84.0 16.4 %all-to-all-start.1 = ((bf16[192,32,16]{0,2,1:T(8,128)(2,1)}), bf16[192,32,16]{0,2,1:T(8,128)(2,1)S(1)}, u32[]{:S(2)}, u32[]{:S(2)}) async-start(bf16[192,32,16]{0,2,1:T(8,128)(2,1)} %bitcast.72), calls=%async_computation.1 | async-start | bytes 524288 | tf_op jit(solution)/shard_map/all_to_all | solution.py:159
  89.8 262.5 %reduce-scatter.2.cloned.1.call-start = ((), (), s32[]{:S(2)}) async-start(), calls=%async_computation.3 | async-start | bytes 1966080 | tf_op jit(solution)/shard_map/reduce_scatter | solution.py:172
  101.6 38.3 %collective-permute-start = (bf16[2192,192]{0,1:T(8,128)(2,1)S(1)}, bf16[2192,192]{0,1:T(8,128)(2,1)S(1)}, u32[]{:S(2)}, u32[]{:S(2)}) collective-permute-start(bf16[2192,192]{0,1:T(8,128)(2,1)S(1)} %fusion.2), channel_id=1, source_target_pairs={{0,4},{4,8},{8,12},{12,16},{16,20},{20,24},{24,28},{28,0},{1,5},{5... | collective-permute-start | bytes 2525192 | tf_op jit(solution)/shard_map/ppermute | solution.py:32
  102.6 39.8 %collective-permute-start.1 = (bf16[2192,192]{0,1:T(8,128)(2,1)S(1)}, bf16[2192,192]{0,1:T(8,128)(2,1)S(1)}, u32[]{:S(2)}, u32[]{:S(2)}) collective-permute-start(bf16[2192,192]{0,1:T(8,128)(2,1)S(1)} %fusion.2), channel_id=1, source_target_pairs={{0,28},{4,0},{8,4},{12,8},{16,12},{20,16},{24,20},{28,24},{1,29},{... | collective-permute-start | bytes 2525192 | tf_op jit(solution)/shard_map/ppermute | solution.py:37
  139.9 38.9 %collective-permute-start.2 = (bf16[2192,192]{0,1:T(8,128)(2,1)S(1)}, bf16[2192,192]{0,1:T(8,128)(2,1)S(1)}, u32[]{:S(2)}, u32[]{:S(2)}) collective-permute-start(bf16[2192,192]{0,1:T(8,128)(2,1)S(1)} %collective-permute-done), channel_id=1, source_target_pairs={{0,4},{4,8},{8,12},{12,16},{16,20},{20,24},{24,28},{28,0},{1,5},{5... | collective-permute-start | bytes 2525192 | tf_op jit(solution)/shard_map/ppermute | solution.py:32
  142.4 38.9 %collective-permute-start.3 = (bf16[2192,192]{0,1:T(8,128)(2,1)S(1)}, bf16[2192,192]{0,1:T(8,128)(2,1)}, u32[]{:S(2)}, u32[]{:S(2)}) collective-permute-start(bf16[2192,192]{0,1:T(8,128)(2,1)S(1)} %collective-permute-done.1), channel_id=1, source_target_pairs={{0,28},{4,0},{8,4},{12,8},{16,12},{20,16},{24,20},{28,24},{1,29},{... | collective-permute-start | bytes 2525192 | tf_op jit(solution)/shard_map/ppermute | solution.py:37
  178.8 38.8 %copy-start = (bf16[2192,192]{0,1:T(8,128)(2,1)}, bf16[2192,192]{0,1:T(8,128)(2,1)S(1)}, u32[]{:S(2)}) copy-start(bf16[2192,192]{0,1:T(8,128)(2,1)S(1)} %collective-permute-done.2) | copy-start | bytes 2525188
  178.8 38.8 %collective-permute-start.4 = (bf16[2192,192]{0,1:T(8,128)(2,1)S(1)}, bf16[2192,192]{0,1:T(8,128)(2,1)S(1)}, u32[]{:S(2)}, u32[]{:S(2)}) collective-permute-start(bf16[2192,192]{0,1:T(8,128)(2,1)S(1)} %collective-permute-done.2), channel_id=1, source_target_pairs={{0,4},{4,8},{8,12},{12,16},{16,20},{20,24},{24,28},{28,0},{1,5},{5... | collective-permute-start | bytes 2525192 | tf_op jit(solution)/shard_map/ppermute | solution.py:32
  181.3 93.4 %collective-permute-start.5 = (bf16[2192,192]{0,1:T(8,128)(2,1)}, bf16[2192,192]{0,1:T(8,128)(2,1)}, u32[]{:S(2)}, u32[]{:S(2)}) collective-permute-start(bf16[2192,192]{0,1:T(8,128)(2,1)} %collective-permute-done.3), channel_id=1, source_target_pairs={{0,28},{4,0},{8,4},{12,8},{16,12},{20,16},{24,20},{28,24},{1,29},{... | collective-permute-start | bytes 2525192 | tf_op jit(solution)/shard_map/ppermute | solution.py:37
  217.6 66.2 %collective-permute-start.6 = (bf16[2192,192]{0,1:T(8,128)(2,1)S(1)}, bf16[2192,192]{0,1:T(8,128)(2,1)}, u32[]{:S(2)}, u32[]{:S(2)}) collective-permute-start(bf16[2192,192]{0,1:T(8,128)(2,1)S(1)} %collective-permute-done.4), channel_id=1, source_target_pairs={{0,4},{4,8},{8,12},{12,16},{16,20},{20,24},{24,28},{28,0},{1,5},{5... | collective-permute-start | bytes 2525192 | tf_op jit(solution)/shard_map/ppermute | solution.py:32
Sparse Core Ops, SparseCore 0:
  324.1 28.1 reduce-scatter.1
